TPU v7x, 32 devices: a whole 2x2x4 slice. The times are simulated.
32 devices in a mesh: diamond: 2 (over x), tile: 16 (over z, y, core).
Axes of the slice: x: 2, y: 2, z: 4, core: 2. Of those that a mesh axis runs over, the one named last changes fastest.
Arguments:
- inputs: bfloat16 [128, 64, 2048], P(None, 'diamond', 'tile'), may hold values from -6 to 6
- cotangent: bfloat16 [128, 64, 2048], P(None, 'diamond', 'tile'), may hold values from -6 to 6
- weight: bfloat16 [7, 128, 128], replicated, may hold values from -0.1875 to 0.1875
- bias: float32 [128], replicated, may hold values from -4 to 4
- ocean: int32 [4, 128], P('diamond', 'tile'), may hold values 0 or 1
Outputs:
- grad_inputs: bfloat16 [128, 64, 2048], P(None, 'diamond', 'tile')
- grad_weight: float32 [7, 128, 128], replicated
- grad_bias: float32 [128], replicated
All inputs are finite; a program needn't handle non-finite values. No bound on the sum of `ocean` on one device may be relied on, other than what follows from the above.
Results may differ from a plain program's by a relative error of at most 0.005.
Values may be sent and summed in bfloat16 or wider, within the bound.
A program may use at most 128 MiB of HBM per device.

v0:
```python
import jax
import jax.numpy as jnp
from jax import lax
from jax.sharding import PartitionSpec as P

BLOCK = 16
OFFSETS = ((0, 0), (0, 1), (0, -1), (1, 0), (-1, 0), (1, -1), (-1, 1))


def extended(value, sides, width):
    for axis, dim in sides:
        size, length = (lax.axis_size(axis), value.shape[dim])
        up = [(i, (i + 1) % size) for i in range(size - 1)]
        down = [(j, i) for i, j in up]
        last = lax.slice_in_dim(value, length - width, length, axis=dim)
        initial = lax.slice_in_dim(value, 0, width, axis=dim)
        before = lax.ppermute(last, axis, up)
        after = lax.ppermute(initial, axis, down)
        value = jnp.concatenate([before, value, after], axis=dim)
    return value


def stacked_taps(padded, rows, cols, sign, base):
    pieces = [
        padded[
            :,
            base + sign * dr : base + sign * dr + rows,
            base + sign * dc : base + sign * dc + cols,
        ]
        for dr, dc in OFFSETS
    ]
    return jnp.stack(pieces, 0)


def pre_grad(taps, weight, bias, grad_here, mask_here):
    feats = weight.shape[1]
    shape_here = grad_here.shape
    flat = taps.reshape(7 * feats, -1)
    pre = (
        lax.dot_general(
            weight.reshape(7 * feats, feats),
            flat,
            (((0,), (0,)), ((), ())),
            preferred_element_type=jnp.float32,
        )
        + bias[:, None]
    )
    sig = jax.nn.sigmoid(pre)
    result = (
        mask_here.reshape(1, -1)
        * grad_here.reshape(feats, -1).astype(jnp.float32)
        * sig
        * (1.0 + pre * (1.0 - sig))
    )
    return result.astype(jnp.bfloat16).reshape(shape_here)


def on_device(inputs, cotangent, weight, bias, ocean):
    feats, rows, cols = inputs.shape
    total_cells = rows * cols * lax.axis_size("diamond") * lax.axis_size("tile")
    scale = total_cells ** (-0.5)
    cell_mask = jnp.repeat(jnp.repeat(ocean.astype(jnp.float32), BLOCK, 0), BLOCK, 1)
    back_weight = jnp.transpose(weight, (1, 0, 2)).reshape(feats, 7 * feats)
    x_pad = extended(inputs, (("diamond", 1), ("tile", 2)), 1)
    taps = stacked_taps(x_pad, rows, cols, 1, 1)
    grad_pre = pre_grad(taps, weight, bias, cotangent, cell_mask)
    taps_inner = taps.reshape(7 * feats, rows * cols)
    grad_inner = grad_pre.reshape(feats, rows * cols)
    grad_region = extended(grad_pre, (("diamond", 1), ("tile", 2)), 1)
    local_w = lax.dot_general(
        taps_inner, grad_inner, (((1,), (1,)), ((), ())), preferred_element_type=jnp.float32
    )
    local_b = jnp.sum(grad_inner.astype(jnp.float32), axis=1)
    sum_w, sum_b = lax.psum((local_w, local_b), ("diamond", "tile"))
    back_taps = stacked_taps(grad_region, rows, cols, -1, 1).reshape(7 * feats, rows * cols)
    total = jnp.dot(back_weight, back_taps, preferred_element_type=jnp.float32)
    grad_inputs = (
        (cotangent.reshape(feats, rows * cols).astype(jnp.float32) + total)
        .astype(jnp.bfloat16)
        .reshape(feats, rows, cols)
    )
    grad_weight = (sum_w * scale).reshape(7, feats, feats)
    grad_bias = sum_b * scale
    return (grad_inputs, grad_weight, grad_bias)


def solution(mesh):
    placed = (
        P(None, "diamond", "tile"),
        P(None, "diamond", "tile"),
        P(),
        P(),
        P("diamond", "tile"),
    )
    return jax.shard_map(
        on_device,
        mesh=mesh,
        in_specs=placed,
        out_specs=(P(None, "diamond", "tile"), P(), P()),
        check_vma=False,
    )
```

profile of v0, /device:TPU:1, one launch (start us, length us, event | category | flops | bytes accessed | tf_op | source)
XLA Modules:
  0.0 196.3 jit_solution(1103404638283157046)
XLA Ops:
  7.2 2.6 %copy.46 = bf16[128,32,128]{0,1,2:T(8,128)(2,1)S(1)} copy(bf16[128,32,128]{2,1,0:T(8,128)(2,1)} %param.5) | data formatting | bytes 2097152 | tf_op args[0]
  10.5 3.9 %collective-permute-start = (bf16[128,1,128]{0,1,2:T(2,128)(2,1)}, bf16[128,1,128]{0,1,2:T(2,128)(2,1)S(1)}, u32[]{:S(2)}, u32[]{:S(2)}) collective-permute-start(bf16[128,1,128]{0,1,2:T(2,128)(2,1)} %get-tuple-element.25), channel_id=1, source_target_pairs={{0,16},{1,17},{2,18},{3,19},{4,20},{5,21},{6,22},{7,23},{8,24},{9,... | collective-permute-start | bytes 98312 | tf_op jit(solution)/shard_map/ppermute | solution.py:17
  18.4 1.9 copy.44
  22.1 2.9 %collective-permute-start.2 = (bf16[128,34,1]{0,1,2:T(8,128)(2,1)S(1)}, bf16[128,34,1]{0,1,2:T(8,128)(2,1)S(1)}, u32[]{:S(2)}, u32[]{:S(2)}) collective-permute-start(bf16[128,34,1]{0,1,2:T(8,128)(2,1)S(1)} %get-tuple-element.22), channel_id=1, source_target_pairs={{1,0},{2,1},{3,2},{4,3},{5,4},{6,5},{7,6},{8,7},{9,8},{10,9},{11,1... | collective-permute-start | bytes 26120 | tf_op jit(solution)/shard_map/ppermute | solution.py:18
  25.4 3.0 %collective-permute-start.3 = (bf16[128,34,1]{0,1,2:T(8,128)(2,1)S(1)}, bf16[128,34,1]{0,1,2:T(8,128)(2,1)S(1)}, u32[]{:S(2)}, u32[]{:S(2)}) collective-permute-start(bf16[128,34,1]{0,1,2:T(8,128)(2,1)S(1)} %get-tuple-element.21), channel_id=1, source_target_pairs={{0,1},{1,2},{2,3},{3,4},{4,5},{5,6},{6,7},{7,8},{8,9},{9,10},{10,1... | collective-permute-start | bytes 26120 | tf_op jit(solution)/shard_map/ppermute | solution.py:17
  28.5 1.4 fusion.50
  33.3 1.4 fusion.45
  34.7 1.3 fusion.43
  36.0 12.3 %copy.57 = bf16[7,128,32,128]{3,2,1,0:T(8,128)(2,1)} copy(bf16[7,128,32,128]{1,3,2,0:T(8,128)(2,1)} %fusion.43) | data formatting | bytes 14680064 | tf_op jit(solution)/shard_map/stack | solution.py:32
  48.3 6.6 %convert_reduce_fusion = (f32[128]{0:T(128)S(1)}, bf16[128,4096]{0,1:T(8,128)(2,1)S(1)}) fusion(f32[128]{0:T(128)S(1)} %copy-done.8, bf16[896,128]{1,0:T(8,128)(2,1)S(1)} %bitcast.116, bf16[112,8,32,128]{3,2,1,0:T(8,128)(2,1)} %bitcast.110, f32[128,32,128]{0,2,1:T(8,128)S(1)} %copy-done.2, f32[4096]{0:T(1024)S(1)} %mul.31), kind=kOutput, calls=%fused_computation.18 | convolution fusion | flops 946339712 | bytes 10732544 | tf_op jit(solution)/shard_map/dot_general | solution.py:40
  55.0 2.9 %fusion.3 = f32[896,128]{1,0:T(8,128)} fusion(bf16[128,4096]{0,1:T(8,128)(2,1)S(1)} %get-tuple-element.28, bf16[112,8,32,128]{3,2,1,0:T(8,128)(2,1)S(1)} %bitcast.111), kind=kOutput, calls=%fused_computation.3 | convolution fusion | flops 939524096 | bytes 8847360 | tf_op jit(solution)/shard_map/dot_general | solution.py:70
  58.7 4.3 %collective-permute-start.4 = (bf16[128,1,128]{0,1,2:T(2,128)(2,1)S(1)}, bf16[128,1,128]{0,1,2:T(2,128)(2,1)S(1)}, u32[]{:S(2)}, u32[]{:S(2)}) collective-permute-start(bf16[128,1,128]{0,1,2:T(2,128)(2,1)S(1)} %get-tuple-element.23), channel_id=1, source_target_pairs={{0,16},{1,17},{2,18},{3,19},{4,20},{5,21},{6,22},{7,23},{8,24},{9,... | collective-permute-start | bytes 98312 | tf_op jit(solution)/shard_map/ppermute | solution.py:17
  64.3 41.4 %psum.15 = f32[128]{0:T(128)S(1)} all-reduce(f32[128]{0:T(128)S(1)} %get-tuple-element.27), channel_id=1, replica_groups=mesh['diamond'=2,'tile'=16] {'diamond','tile'}, use_global_device_ids=true, to_apply=%region_2.0 | all-reduce | flops 128 | bytes 1024 | tf_op jit(solution)/shard_map/psum | solution.py:74
  108.1 5.1 %collective-permute-start.6 = (bf16[128,34,1]{0,1,2:T(8,128)(2,1)S(1)}, bf16[128,34,1]{0,1,2:T(8,128)(2,1)S(1)}, u32[]{:S(2)}, u32[]{:S(2)}) collective-permute-start(bf16[128,34,1]{0,1,2:T(8,128)(2,1)S(1)} %get-tuple-element.20), channel_id=1, source_target_pairs={{0,1},{1,2},{2,3},{3,4},{4,5},{5,6},{6,7},{7,8},{8,9},{9,10},{10,1... | collective-permute-start | bytes 26120 | tf_op jit(solution)/shard_map/ppermute | solution.py:17
  113.5 1.9 collective-permute-start.7
  115.5 1.4 fusion.31
  116.9 2.0 %collective-permute-done.7 = bf16[128,34,1]{0,1,2:T(8,128)(2,1)S(1)} collective-permute-done((bf16[128,34,1]{0,1,2:T(8,128)(2,1)S(1)}, bf16[128,34,1]{0,1,2:T(8,128)(2,1)S(1)}, u32[]{:S(2)}, u32[]{:S(2)}) %collective-permute-start.7) | collective-permute-done | bytes 8736 | tf_op jit(solution)/shard_map/ppermute | solution.py:18
  119.0 1.4 fusion.42
  122.4 1.4 fusion.37
  125.1 12.4 %copy.67 = bf16[7,128,32,128]{3,2,1,0:T(8,128)(2,1)} copy(bf16[7,128,32,128]{1,3,2,0:T(8,128)(2,1)} %fusion.36) | data formatting | bytes 14680064 | tf_op jit(solution)/shard_map/stack | solution.py:32
  137.5 9.5 %fusion.21 = bf16[128,4096]{0,1:T(8,128)(2,1)S(1)} fusion(f32[128,4096]{0,1:T(8,128)S(1)} %bitcast.113, bf16[128,896]{0,1:T(8,128)(2,1)S(1)} %bitcast.117, bf16[112,8,32,128]{3,2,1,0:T(8,128)(2,1)} %bitcast.112), kind=kOutput, calls=%fused_computation.13 | convolution fusion | flops 940572672 | bytes 10715136 | tf_op jit(solution)/shard_map/dot_general | solution.py:76
  147.0 1.7 copy.69
  148.7 38.9 %all-reduce.2.cloned.1.call-done = f32[896,128]{1,0:T(8,128)} async-done(((f32[896,128]{1,0:T(8,128)}), f32[896,128]{1,0:T(8,128)}) %all-reduce.2.cloned.1.call-update) | async-done | bytes 458768 | tf_op jit(solution)/shard_map/psum | solution.py:74
  187.6 1.8 broadcast_multiply_fusion
  (61 shorter events, 18.7 us)
Async XLA Ops:
  7.2 8.6 %copy-start.1 = (bf16[128,32,128]{2,1,0:T(8,128)(2,1)S(1)}, bf16[128,32,128]{2,1,0:T(8,128)(2,1)}, u32[]{:S(2)}) copy-start(bf16[128,32,128]{2,1,0:T(8,128)(2,1)} %param.5) | copy-start | bytes 3145732
  7.2 180.5 %all-reduce.2.cloned.1.call-start = ((), (), s32[]{:S(2)}) async-start(), calls=%async_computation | async-start | bytes 917504 | tf_op jit(solution)/shard_map/psum | solution.py:74
  10.5 10.8 %collective-permute-start = (bf16[128,1,128]{0,1,2:T(2,128)(2,1)}, bf16[128,1,128]{0,1,2:T(2,128)(2,1)S(1)}, u32[]{:S(2)}, u32[]{:S(2)}) collective-permute-start(bf16[128,1,128]{0,1,2:T(2,128)(2,1)} %get-tuple-element.25), channel_id=1, source_target_pairs={{0,16},{1,17},{2,18},{3,19},{4,20},{5,21},{6,22},{7,23},{8,24},{9,... | collective-permute-start | bytes 98312 | tf_op jit(solution)/shard_map/ppermute | solution.py:17
  14.5 6.9 %collective-permute-start.1 = (bf16[128,1,128]{0,1,2:T(2,128)(2,1)}, bf16[128,1,128]{0,1,2:T(2,128)(2,1)S(1)}, u32[]{:S(2)}, u32[]{:S(2)}) collective-permute-start(bf16[128,1,128]{0,1,2:T(2,128)(2,1)} %get-tuple-element.26), channel_id=1, source_target_pairs={{16,0},{17,1},{18,2},{19,3},{20,4},{21,5},{22,6},{23,7},{24,8},{25... | collective-permute-start | bytes 98312 | tf_op jit(solution)/shard_map/ppermute | solution.py:18
  16.8 1.6 copy-start.4
  16.8 3.5 %copy-start.7 = (s32[2,8]{1,0:T(2,128)S(1)}, s32[2,8]{1,0:T(2,128)}, u32[]{:S(2)}) copy-start(s32[2,8]{1,0:T(2,128)} %param.9) | copy-start | bytes 196
  18.4 2.1 %copy-start.5 = (bf16[7,128,128]{2,1,0:T(8,128)(2,1)S(1)}, bf16[7,128,128]{2,1,0:T(8,128)(2,1)}, u32[]{:S(2)}) copy-start(bf16[7,128,128]{2,1,0:T(8,128)(2,1)} %param.7) | copy-start | bytes 688132
  22.1 6.3 %collective-permute-start.2 = (bf16[128,34,1]{0,1,2:T(8,128)(2,1)S(1)}, bf16[128,34,1]{0,1,2:T(8,128)(2,1)S(1)}, u32[]{:S(2)}, u32[]{:S(2)}) collective-permute-start(bf16[128,34,1]{0,1,2:T(8,128)(2,1)S(1)} %get-tuple-element.22), channel_id=1, source_target_pairs={{1,0},{2,1},{3,2},{4,3},{5,4},{6,5},{7,6},{8,7},{9,8},{10,9},{11,1... | collective-permute-start | bytes 26120 | tf_op jit(solution)/shard_map/ppermute | solution.py:18
  25.4 4.5 %collective-permute-start.3 = (bf16[128,34,1]{0,1,2:T(8,128)(2,1)S(1)}, bf16[128,34,1]{0,1,2:T(8,128)(2,1)S(1)}, u32[]{:S(2)}, u32[]{:S(2)}) collective-permute-start(bf16[128,34,1]{0,1,2:T(8,128)(2,1)S(1)} %get-tuple-element.21), channel_id=1, source_target_pairs={{0,1},{1,2},{2,3},{3,4},{4,5},{5,6},{6,7},{7,8},{8,9},{9,10},{10,1... | collective-permute-start | bytes 26120 | tf_op jit(solution)/shard_map/ppermute | solution.py:17
  36.0 12.3 %copy-start.2 = (f32[128,32,128]{0,2,1:T(8,128)S(1)}, f32[128,32,128]{0,2,1:T(8,128)}, u32[]{:S(2)}) copy-start(f32[128,32,128]{0,2,1:T(8,128)} %copy.44) | copy-start | bytes 6291460
  36.0 12.3 %copy-start.8 = (f32[128]{0:T(128)S(1)}, f32[128]{0:T(128)}, u32[]{:S(2)}) copy-start(f32[128]{0:T(128)} %param.8) | copy-start | bytes 1540
  48.3 6.6 %copy-start = (bf16[7,128,32,128]{3,2,1,0:T(8,128)(2,1)S(1)}, bf16[7,128,32,128]{3,2,1,0:T(8,128)(2,1)}, u32[]{:S(2)}) copy-start(bf16[7,128,32,128]{3,2,1,0:T(8,128)(2,1)} %copy.57) | copy-start | bytes 22020100
  58.7 48.6 %collective-permute-start.4 = (bf16[128,1,128]{0,1,2:T(2,128)(2,1)S(1)}, bf16[128,1,128]{0,1,2:T(2,128)(2,1)S(1)}, u32[]{:S(2)}, u32[]{:S(2)}) collective-permute-start(bf16[128,1,128]{0,1,2:T(2,128)(2,1)S(1)} %get-tuple-element.23), channel_id=1, source_target_pairs={{0,16},{1,17},{2,18},{3,19},{4,20},{5,21},{6,22},{7,23},{8,24},{9,... | collective-permute-start | bytes 98312 | tf_op jit(solution)/shard_map/ppermute | solution.py:17
  63.0 44.3 %collective-permute-start.5 = (bf16[128,1,128]{0,1,2:T(2,128)(2,1)S(1)}, bf16[128,1,128]{0,1,2:T(2,128)(2,1)S(1)}, u32[]{:S(2)}, u32[]{:S(2)}) collective-permute-start(bf16[128,1,128]{0,1,2:T(2,128)(2,1)S(1)} %get-tuple-element.24), channel_id=1, source_target_pairs={{16,0},{17,1},{18,2},{19,3},{20,4},{21,5},{22,6},{23,7},{24,8},{25... | collective-permute-start | bytes 98312 | tf_op jit(solution)/shard_map/ppermute | solution.py:18
  108.1 7.4 %collective-permute-start.6 = (bf16[128,34,1]{0,1,2:T(8,128)(2,1)S(1)}, bf16[128,34,1]{0,1,2:T(8,128)(2,1)S(1)}, u32[]{:S(2)}, u32[]{:S(2)}) collective-permute-start(bf16[128,34,1]{0,1,2:T(8,128)(2,1)S(1)} %get-tuple-element.20), channel_id=1, source_target_pairs={{0,1},{1,2},{2,3},{3,4},{4,5},{5,6},{6,7},{7,8},{8,9},{9,10},{10,1... | collective-permute-start | bytes 26120 | tf_op jit(solution)/shard_map/ppermute | solution.py:17
  113.5 5.4 %collective-permute-start.7 = (bf16[128,34,1]{0,1,2:T(8,128)(2,1)S(1)}, bf16[128,34,1]{0,1,2:T(8,128)(2,1)S(1)}, u32[]{:S(2)}, u32[]{:S(2)}) collective-permute-start(bf16[128,34,1]{0,1,2:T(8,128)(2,1)S(1)} %get-tuple-element.19), channel_id=1, source_target_pairs={{1,0},{2,1},{3,2},{4,3},{5,4},{6,5},{7,6},{8,7},{9,8},{10,9},{11,1... | collective-permute-start | bytes 26120 | tf_op jit(solution)/shard_map/ppermute | solution.py:18
  125.1 12.4 %copy-start.3 = (f32[128,32,128]{0,2,1:T(8,128)S(1)}, f32[128,32,128]{0,2,1:T(8,128)}, u32[]{:S(2)}) copy-start(f32[128,32,128]{0,2,1:T(8,128)} %copy.44) | copy-start | bytes 6291460
  125.1 12.4 %copy-start.6 = (bf16[7,128,128]{1,2,0:T(8,128)(2,1)S(1)}, bf16[7,128,128]{1,2,0:T(8,128)(2,1)}, u32[]{:S(2)}) copy-start(bf16[7,128,128]{1,2,0:T(8,128)(2,1)} %copy.68) | copy-start | bytes 688132
Sparse Core Ops, SparseCore 0:
  58.0 129.5 all-reduce.1
where the time goes:
time: 197 us; the launch traced here: 196 us
  local copies, waits for them, and re-layouts  43.3 us (22%)
  blocking collectives  41.4 us (21%)
  waiting for transfers between devices  41 us (21%)
  starting transfers between devices  23.7 us (12%)
  matrix products  19 us (10%)
  between operations  14.3 us (7%)
  other arithmetic  13.6 us (7%)
    psum x1, blocking collectives, on_device(): sum_w, sum_b = lax.psum((local_w, local_b), ('diamond', 'tile'))  41.4 us
    psum x1, waiting for transfers between devices, on_device(): sum_w, sum_b = lax.psum((local_w, local_b), ('diamond', 'tile'))  38.9 us
    another operation x3, local copies, waits for them, and re-layouts, stacked_taps(): return jnp.stack(pieces, 0)  26 us
    ppermute x4, starting transfers between devices, extended(): before = lax.ppermute(last, axis, up)  16.3 us
    unnamed x29, local copies, waits for them, and re-layouts  13.6 us
    dot_general x1, matrix products, on_device(): total = jnp.dot(back_weight, back_taps, preferred_element_type=jnp.float32)  9.47 us
    unnamed x7, other arithmetic  8.35 us
    ppermute x4, starting transfers between devices, extended(): after = lax.ppermute(initial, axis, down)  7.37 us
  transfers between devices with their start and end apart: 9, of which 2 were waited for; matrix products, arithmetic and copies ran while one was open for 21% of the time, Pallas kernels for 0%

commit v1 on v0

--- a/solution.py
+++ b/solution.py
@@ -71,7 +71,7 @@
         taps_inner, grad_inner, (((1,), (1,)), ((), ())), preferred_element_type=jnp.float32
     )
     local_b = jnp.sum(grad_inner.astype(jnp.float32), axis=1)
-    sum_w, sum_b = lax.psum((local_w, local_b), ("diamond", "tile"))
+    sum_w, sum_b = lax.psum(lax.psum((local_w, local_b), "tile"), "diamond")
     back_taps = stacked_taps(grad_region, rows, cols, -1, 1).reshape(7 * feats, rows * cols)
     total = jnp.dot(back_weight, back_taps, preferred_element_type=jnp.float32)
     grad_inputs = (

time: 197 us -> 190 us (0.964)
  blocking collectives: 41.4 us -> 35.2 us
    psum x1 -> x2, blocking collectives: 41.4 us -> 35.2 us  [on_device(): sum_w, sum_b = lax.psum(lax.psum((local_w, local_b), 'tile'), 'diamond')]
    ppermute x4, starting transfers between devices: 16.3 us -> 13.2 us  [extended(): before = lax.ppermute(last, axis, up)]
    ppermute x4, starting transfers between devices: 7.37 us -> 9.75 us  [extended(): after = lax.ppermute(initial, axis, down)]
    ppermute x4, waiting for transfers between devices: 2 us -> 0.01 us  [extended(): after = lax.ppermute(initial, axis, down)]
    psum x1 -> x2, waiting for transfers between devices: 38.9 us -> 40.4 us  [on_device(): sum_w, sum_b = lax.psum(lax.psum((local_w, local_b), 'tile'), 'diamond')]
  transfers between devices with their start and end apart: 9 -> 10, of which waited for: 2 -> 2; matrix products, arithmetic and copies ran while one was open for 21% -> 22% of each run, Pallas kernels for 0% -> 0%
where the time goes in v1:
time: 190 us; the launch traced here: 189 us
  local copies, waits for them, and re-layouts  43.3 us (23%)
  waiting for transfers between devices  40.5 us (21%)
  blocking collectives  35.2 us (19%)
  starting transfers between devices  23 us (12%)
  matrix products  19 us (10%)
  between operations  14.4 us (8%)
  other arithmetic  13.6 us (7%)
    psum x2, waiting for transfers between devices, on_device(): sum_w, sum_b = lax.psum(lax.psum((local_w, local_b), 'tile'), 'diamond')  40.4 us
    psum x2, blocking collectives, on_device(): sum_w, sum_b = lax.psum(lax.psum((local_w, local_b), 'tile'), 'diamond')  35.2 us
    another operation x3, local copies, waits for them, and re-layouts, stacked_taps(): return jnp.stack(pieces, 0)  26 us
    unnamed x29, local copies, waits for them, and re-layouts  13.5 us
    ppermute x4, starting transfers between devices, extended(): before = lax.ppermute(last, axis, up)  13.2 us
    ppermute x4, starting transfers between devices, extended(): after = lax.ppermute(initial, axis, down)  9.75 us
    dot_general x1, matrix products, on_device(): total = jnp.dot(back_weight, back_taps, preferred_element_type=jnp.float32)  9.48 us
    unnamed x7, other arithmetic  8.35 us
  transfers between devices with their start and end apart: 10, of which 2 were waited for; matrix products, arithmetic and copies ran while one was open for 22% of the time, Pallas kernels for 0%

profile of v1, /device:TPU:1, one launch (start us, length us, event | category | flops | bytes accessed | tf_op | source)
XLA Modules:
  0.0 188.9 jit_solution(16079318652993024365)
XLA Ops:
  7.2 2.6 %copy.46 = bf16[128,32,128]{0,1,2:T(8,128)(2,1)S(1)} copy(bf16[128,32,128]{2,1,0:T(8,128)(2,1)} %param.5) | data formatting | bytes 2097152 | tf_op args[0]
  10.5 3.9 %collective-permute-start = (bf16[128,1,128]{0,1,2:T(2,128)(2,1)}, bf16[128,1,128]{0,1,2:T(2,128)(2,1)S(1)}, u32[]{:S(2)}, u32[]{:S(2)}) collective-permute-start(bf16[128,1,128]{0,1,2:T(2,128)(2,1)} %get-tuple-element.25), channel_id=1, source_target_pairs={{0,16},{1,17},{2,18},{3,19},{4,20},{5,21},{6,22},{7,23},{8,24},{9,... | collective-permute-start | bytes 98312 | tf_op jit(solution)/shard_map/ppermute | solution.py:17
  18.4 1.9 %copy.44 = f32[128,32,128]{0,2,1:T(8,128)} copy(bf16[128,32,128]{2,1,0:T(8,128)(2,1)S(1)} %copy-done.4) | data formatting | bytes 3145728 | tf_op jit(solution)/shard_map/convert_element_type | solution.py:78
  22.1 2.9 %collective-permute-start.2 = (bf16[128,34,1]{0,1,2:T(8,128)(2,1)S(1)}, bf16[128,34,1]{0,1,2:T(8,128)(2,1)S(1)}, u32[]{:S(2)}, u32[]{:S(2)}) collective-permute-start(bf16[128,34,1]{0,1,2:T(8,128)(2,1)S(1)} %get-tuple-element.22), channel_id=1, source_target_pairs={{1,0},{2,1},{3,2},{4,3},{5,4},{6,5},{7,6},{8,7},{9,8},{10,9},{11,1... | collective-permute-start | bytes 26120 | tf_op jit(solution)/shard_map/ppermute | solution.py:18
  25.4 3.0 %collective-permute-start.3 = (bf16[128,34,1]{0,1,2:T(8,128)(2,1)S(1)}, bf16[128,34,1]{0,1,2:T(8,128)(2,1)S(1)}, u32[]{:S(2)}, u32[]{:S(2)}) collective-permute-start(bf16[128,34,1]{0,1,2:T(8,128)(2,1)S(1)} %get-tuple-element.21), channel_id=1, source_target_pairs={{0,1},{1,2},{2,3},{3,4},{4,5},{5,6},{6,7},{7,8},{8,9},{9,10},{10,1... | collective-permute-start | bytes 26120 | tf_op jit(solution)/shard_map/ppermute | solution.py:17
  28.5 1.4 fusion.50
  33.3 1.4 fusion.45
  34.7 1.4 fusion.43
  36.0 12.3 %copy.57 = bf16[7,128,32,128]{3,2,1,0:T(8,128)(2,1)} copy(bf16[7,128,32,128]{1,3,2,0:T(8,128)(2,1)} %fusion.43) | data formatting | bytes 14680064 | tf_op jit(solution)/shard_map/stack | solution.py:32
  48.4 6.6 %convert_reduce_fusion = (f32[128]{0:T(128)S(1)}, bf16[128,4096]{0,1:T(8,128)(2,1)S(1)}) fusion(f32[128]{0:T(128)S(1)} %copy-done.8, bf16[896,128]{1,0:T(8,128)(2,1)S(1)} %bitcast.116, bf16[112,8,32,128]{3,2,1,0:T(8,128)(2,1)} %bitcast.111, f32[128,32,128]{0,2,1:T(8,128)S(1)} %copy-done.2, f32[4096]{0:T(1024)S(1)} %mul.31), kind=kOutput, calls=%fused_computation.18 | convolution fusion | flops 946339712 | bytes 10732544 | tf_op jit(solution)/shard_map/dot_general | solution.py:40
  55.0 2.9 %fusion.3 = f32[896,128]{1,0:T(8,128)} fusion(bf16[128,4096]{0,1:T(8,128)(2,1)S(1)} %get-tuple-element.28, bf16[112,8,32,128]{3,2,1,0:T(8,128)(2,1)S(1)} %bitcast.112), kind=kOutput, calls=%fused_computation.3 | convolution fusion | flops 939524096 | bytes 8847360 | tf_op jit(solution)/shard_map/dot_general | solution.py:70
  58.8 4.3 %collective-permute-start.4 = (bf16[128,1,128]{0,1,2:T(2,128)(2,1)S(1)}, bf16[128,1,128]{0,1,2:T(2,128)(2,1)S(1)}, u32[]{:S(2)}, u32[]{:S(2)}) collective-permute-start(bf16[128,1,128]{0,1,2:T(2,128)(2,1)S(1)} %get-tuple-element.23), channel_id=1, source_target_pairs={{0,16},{1,17},{2,18},{3,19},{4,20},{5,21},{6,22},{7,23},{8,24},{9,... | collective-permute-start | bytes 98312 | tf_op jit(solution)/shard_map/ppermute | solution.py:17
  64.4 30.0 %psum.30 = f32[128]{0:T(128)S(1)} all-reduce(f32[128]{0:T(128)S(1)} %get-tuple-element.27), channel_id=1, replica_groups=mesh['diamond'=2,'tile'=16] {'tile'}, use_global_device_ids=true, to_apply=%region_3.0 | all-reduce | flops 128 | bytes 1024 | tf_op jit(solution)/shard_map/psum | solution.py:74
  94.3 5.2 %psum.31 = f32[128]{0:T(128)S(1)} all-reduce(f32[128]{0:T(128)S(1)} %psum.30), channel_id=1, replica_groups=mesh['diamond'=2,'tile'=16] {'diamond'}, use_global_device_ids=true, to_apply=%region_4.0 | all-reduce | flops 128 | bytes 1024 | tf_op jit(solution)/shard_map/psum | solution.py:74
  102.0 1.9 %collective-permute-start.6 = (bf16[128,34,1]{0,1,2:T(8,128)(2,1)S(1)}, bf16[128,34,1]{0,1,2:T(8,128)(2,1)S(1)}, u32[]{:S(2)}, u32[]{:S(2)}) collective-permute-start(bf16[128,34,1]{0,1,2:T(8,128)(2,1)S(1)} %get-tuple-element.20), channel_id=1, source_target_pairs={{0,1},{1,2},{2,3},{3,4},{4,5},{5,6},{6,7},{7,8},{8,9},{9,10},{10,1... | collective-permute-start | bytes 26120 | tf_op jit(solution)/shard_map/ppermute | solution.py:17
  104.2 4.3 %collective-permute-start.7 = (bf16[128,34,1]{0,1,2:T(8,128)(2,1)S(1)}, bf16[128,34,1]{0,1,2:T(8,128)(2,1)S(1)}, u32[]{:S(2)}, u32[]{:S(2)}) collective-permute-start(bf16[128,34,1]{0,1,2:T(8,128)(2,1)S(1)} %get-tuple-element.19), channel_id=1, source_target_pairs={{1,0},{2,1},{3,2},{4,3},{5,4},{6,5},{7,6},{8,7},{9,8},{10,9},{11,1... | collective-permute-start | bytes 26120 | tf_op jit(solution)/shard_map/ppermute | solution.py:18
  108.6 1.4 fusion.31
  113.5 1.4 fusion.37
  116.3 12.3 %copy.67 = bf16[7,128,32,128]{3,2,1,0:T(8,128)(2,1)} copy(bf16[7,128,32,128]{1,3,2,0:T(8,128)(2,1)} %fusion.36) | data formatting | bytes 14680064 | tf_op jit(solution)/shard_map/stack | solution.py:32
  128.6 22.3 %all-reduce.3.cloned.1.call-done = f32[896,128]{1,0:T(8,128)} async-done(((f32[896,128]{1,0:T(8,128)}), f32[896,128]{1,0:T(8,128)}) %all-reduce.3.cloned.1.call-update) | async-done | bytes 458768 | tf_op jit(solution)/shard_map/psum | solution.py:74
  150.9 9.5 %fusion.21 = bf16[128,4096]{0,1:T(8,128)(2,1)S(1)} fusion(f32[128,4096]{0,1:T(8,128)S(1)} %bitcast.113, bf16[128,896]{0,1:T(8,128)(2,1)S(1)} %bitcast.117, bf16[112,8,32,128]{3,2,1,0:T(8,128)(2,1)} %bitcast.110), kind=kOutput, calls=%fused_computation.13 | convolution fusion | flops 940572672 | bytes 10715136 | tf_op jit(solution)/shard_map/dot_general | solution.py:76
  160.4 1.7 copy.69
  162.1 18.1 %all-reduce.5.cloned.1.call-done = f32[896,128]{1,0:T(8,128)} async-done(((f32[896,128]{1,0:T(8,128)}), f32[896,128]{1,0:T(8,128)}) %all-reduce.5.cloned.1.call-update) | async-done | bytes 458768 | tf_op jit(solution)/shard_map/psum | solution.py:74
  180.2 1.8 broadcast_multiply_fusion
  (65 shorter events, 20.1 us)
Async XLA Ops:
  7.2 8.6 %copy-start.1 = (bf16[128,32,128]{2,1,0:T(8,128)(2,1)S(1)}, bf16[128,32,128]{2,1,0:T(8,128)(2,1)}, u32[]{:S(2)}) copy-start(bf16[128,32,128]{2,1,0:T(8,128)(2,1)} %param.5) | copy-start | bytes 3145732
  7.2 143.7 %all-reduce.3.cloned.1.call-start = ((), (), s32[]{:S(2)}) async-start(), calls=%async_computation | async-start | bytes 917504 | tf_op jit(solution)/shard_map/psum | solution.py:74
  10.5 10.8 %collective-permute-start = (bf16[128,1,128]{0,1,2:T(2,128)(2,1)}, bf16[128,1,128]{0,1,2:T(2,128)(2,1)S(1)}, u32[]{:S(2)}, u32[]{:S(2)}) collective-permute-start(bf16[128,1,128]{0,1,2:T(2,128)(2,1)} %get-tuple-element.25), channel_id=1, source_target_pairs={{0,16},{1,17},{2,18},{3,19},{4,20},{5,21},{6,22},{7,23},{8,24},{9,... | collective-permute-start | bytes 98312 | tf_op jit(solution)/shard_map/ppermute | solution.py:17
  14.5 6.9 %collective-permute-start.1 = (bf16[128,1,128]{0,1,2:T(2,128)(2,1)}, bf16[128,1,128]{0,1,2:T(2,128)(2,1)S(1)}, u32[]{:S(2)}, u32[]{:S(2)}) collective-permute-start(bf16[128,1,128]{0,1,2:T(2,128)(2,1)} %get-tuple-element.26), channel_id=1, source_target_pairs={{16,0},{17,1},{18,2},{19,3},{20,4},{21,5},{22,6},{23,7},{24,8},{25... | collective-permute-start | bytes 98312 | tf_op jit(solution)/shard_map/ppermute | solution.py:18
  16.8 1.6 copy-start.4
  16.8 3.5 %copy-start.7 = (s32[2,8]{1,0:T(2,128)S(1)}, s32[2,8]{1,0:T(2,128)}, u32[]{:S(2)}) copy-start(s32[2,8]{1,0:T(2,128)} %param.9) | copy-start | bytes 196
  18.4 2.1 %copy-start.5 = (bf16[7,128,128]{2,1,0:T(8,128)(2,1)S(1)}, bf16[7,128,128]{2,1,0:T(8,128)(2,1)}, u32[]{:S(2)}) copy-start(bf16[7,128,128]{2,1,0:T(8,128)(2,1)} %param.7) | copy-start | bytes 688132
  22.1 6.3 %collective-permute-start.2 = (bf16[128,34,1]{0,1,2:T(8,128)(2,1)S(1)}, bf16[128,34,1]{0,1,2:T(8,128)(2,1)S(1)}, u32[]{:S(2)}, u32[]{:S(2)}) collective-permute-start(bf16[128,34,1]{0,1,2:T(8,128)(2,1)S(1)} %get-tuple-element.22), channel_id=1, source_target_pairs={{1,0},{2,1},{3,2},{4,3},{5,4},{6,5},{7,6},{8,7},{9,8},{10,9},{11,1... | collective-permute-start | bytes 26120 | tf_op jit(solution)/shard_map/ppermute | solution.py:18
  25.4 4.5 %collective-permute-start.3 = (bf16[128,34,1]{0,1,2:T(8,128)(2,1)S(1)}, bf16[128,34,1]{0,1,2:T(8,128)(2,1)S(1)}, u32[]{:S(2)}, u32[]{:S(2)}) collective-permute-start(bf16[128,34,1]{0,1,2:T(8,128)(2,1)S(1)} %get-tuple-element.21), channel_id=1, source_target_pairs={{0,1},{1,2},{2,3},{3,4},{4,5},{5,6},{6,7},{7,8},{8,9},{9,10},{10,1... | collective-permute-start | bytes 26120 | tf_op jit(solution)/shard_map/ppermute | solution.py:17
  36.0 12.3 %copy-start.2 = (f32[128,32,128]{0,2,1:T(8,128)S(1)}, f32[128,32,128]{0,2,1:T(8,128)}, u32[]{:S(2)}) copy-start(f32[128,32,128]{0,2,1:T(8,128)} %copy.44) | copy-start | bytes 6291460
  36.0 12.3 %copy-start.8 = (f32[128]{0:T(128)S(1)}, f32[128]{0:T(128)}, u32[]{:S(2)}) copy-start(f32[128]{0:T(128)} %param.8) | copy-start | bytes 1540
  48.4 6.6 %copy-start = (bf16[7,128,32,128]{3,2,1,0:T(8,128)(2,1)S(1)}, bf16[7,128,32,128]{3,2,1,0:T(8,128)(2,1)}, u32[]{:S(2)}) copy-start(bf16[7,128,32,128]{3,2,1,0:T(8,128)(2,1)} %copy.57) | copy-start | bytes 22020100
  57.9 122.3 %all-reduce.5.cloned.1.call-start = ((), (), s32[]{:S(2)}) async-start(), calls=%async_computation.1 | async-start | bytes 917504 | tf_op jit(solution)/shard_map/psum | solution.py:74
  58.8 42.4 %collective-permute-start.4 = (bf16[128,1,128]{0,1,2:T(2,128)(2,1)S(1)}, bf16[128,1,128]{0,1,2:T(2,128)(2,1)S(1)}, u32[]{:S(2)}, u32[]{:S(2)}) collective-permute-start(bf16[128,1,128]{0,1,2:T(2,128)(2,1)S(1)} %get-tuple-element.23), channel_id=1, source_target_pairs={{0,16},{1,17},{2,18},{3,19},{4,20},{5,21},{6,22},{7,23},{8,24},{9,... | collective-permute-start | bytes 98312 | tf_op jit(solution)/shard_map/ppermute | solution.py:17
  63.1 38.1 %collective-permute-start.5 = (bf16[128,1,128]{0,1,2:T(2,128)(2,1)S(1)}, bf16[128,1,128]{0,1,2:T(2,128)(2,1)S(1)}, u32[]{:S(2)}, u32[]{:S(2)}) collective-permute-start(bf16[128,1,128]{0,1,2:T(2,128)(2,1)S(1)} %get-tuple-element.24), channel_id=1, source_target_pairs={{16,0},{17,1},{18,2},{19,3},{20,4},{21,5},{22,6},{23,7},{24,8},{25... | collective-permute-start | bytes 98312 | tf_op jit(solution)/shard_map/ppermute | solution.py:18
  102.0 6.6 %collective-permute-start.6 = (bf16[128,34,1]{0,1,2:T(8,128)(2,1)S(1)}, bf16[128,34,1]{0,1,2:T(8,128)(2,1)S(1)}, u32[]{:S(2)}, u32[]{:S(2)}) collective-permute-start(bf16[128,34,1]{0,1,2:T(8,128)(2,1)S(1)} %get-tuple-element.20), channel_id=1, source_target_pairs={{0,1},{1,2},{2,3},{3,4},{4,5},{5,6},{6,7},{7,8},{8,9},{9,10},{10,1... | collective-permute-start | bytes 26120 | tf_op jit(solution)/shard_map/ppermute | solution.py:17
  104.2 5.8 %collective-permute-start.7 = (bf16[128,34,1]{0,1,2:T(8,128)(2,1)S(1)}, bf16[128,34,1]{0,1,2:T(8,128)(2,1)S(1)}, u32[]{:S(2)}, u32[]{:S(2)}) collective-permute-start(bf16[128,34,1]{0,1,2:T(8,128)(2,1)S(1)} %get-tuple-element.19), channel_id=1, source_target_pairs={{1,0},{2,1},{3,2},{4,3},{5,4},{6,5},{7,6},{8,7},{9,8},{10,9},{11,1... | collective-permute-start | bytes 26120 | tf_op jit(solution)/shard_map/ppermute | solution.py:18
  116.3 34.6 %copy-start.3 = (f32[128,32,128]{0,2,1:T(8,128)S(1)}, f32[128,32,128]{0,2,1:T(8,128)}, u32[]{:S(2)}) copy-start(f32[128,32,128]{0,2,1:T(8,128)} %copy.44) | copy-start | bytes 6291460
  116.3 34.6 %copy-start.6 = (bf16[7,128,128]{1,2,0:T(8,128)(2,1)S(1)}, bf16[7,128,128]{1,2,0:T(8,128)(2,1)}, u32[]{:S(2)}) copy-start(bf16[7,128,128]{1,2,0:T(8,128)(2,1)} %copy.68) | copy-start | bytes 688132
Sparse Core Ops, SparseCore 0:
  58.1 92.7 all-reduce.2
  153.2 27.0 all-reduce.4
